TPU v7x, 256 devices: a whole 4x4x8 slice. The times are simulated.
256 devices in a mesh: section: 16 (over z_lo, x), ctx: 16 (over z_hi, y, core).
Axes of the slice: x: 4, y: 4, z: 8 (z_hi: 2, z_lo: 4; z = z_hi * 4 + z_lo), core: 2. Of those that a mesh axis runs over, the one named last changes fastest.
Arguments:
- queries: bfloat16 [16, 4096, 16, 128], P('section', 'ctx'), may hold values from -12 to 12
- keys: bfloat16 [16, 4096, 128], P('section', 'ctx'), may hold values from -6 to 6
- values: bfloat16 [16, 4096, 128], P('section', 'ctx'), may hold values from -6 to 6
- outputs: bfloat16 [16, 4096, 16, 128], P('section', 'ctx'), may hold values from -6 to 6, as said below
- grad_held: bfloat16 [16, 4096, 16, 128], P('section', 'ctx'), may hold values from -24 to 24
- lse: float32 [16, 16, 4096], P('section', None, 'ctx'), as said below
- span_start: int32 [32], replicated, may hold values from 0 to 3968, as said below
Outputs:
- query_grad: bfloat16 [16, 4096, 16, 128], P('section', 'ctx')
- key_grad: bfloat16 [16, 4096, 128], P('section', 'ctx')
- value_grad: bfloat16 [16, 4096, 128], P('section', 'ctx')
Inputs may be any that keep to these rules, and one draw needn't show every extreme that they name: `span_start`: each multiple of 128 below 4096 appears once. Entries 2 k and 2 k + 1 are the spans held by index k of ctx; they add up to 3968, the smaller first. lse[s, h, i] is the log of the sum of exp(scores[s, h, i, j]) over the j with positions[j] <= positions[i]. outputs[s, i, h] is the sum over j of probs[s, h, i, j] values[s, j], rounded once.
All inputs are finite; a program needn't handle non-finite values.
Results may differ from a plain program's by a relative error of at most 0.014.
Values may be sent and summed in bfloat16 or wider, within the bound.
A program may use at most 64 MiB of HBM per device.

v0:
```python
import jax
import jax.numpy as jnp
from jax import lax
from jax.sharding import PartitionSpec as P


def from_behind(shard, axis, by):
    length = lax.axis_size(axis)
    return lax.ppermute(shard, axis, [(i, (i + by) % length) for i in range(length)])


def tile_grads(
    query_rows, grad_rows, lse_rows, delta_rows, query_pos, key_rows, value_rows, key_pos
):
    score_scale = query_rows.shape[-1] ** (-0.5)
    scores = (
        jnp.einsum("rhd,cd->hrc", query_rows, key_rows, preferred_element_type=jnp.float32)
        * score_scale
    )
    allowed = key_pos[None, :] <= query_pos[:, None]
    probs = jnp.where(allowed[None], jnp.exp(scores - lse_rows[:, :, None]), 0.0)
    probs_low = probs.astype(jnp.bfloat16)
    grad_probs = jnp.einsum(
        "rhd,cd->hrc", grad_rows, value_rows, preferred_element_type=jnp.float32
    )
    grad_scores = (probs * (grad_probs - delta_rows[:, :, None])).astype(jnp.bfloat16)
    query_grad = (
        jnp.einsum("hrc,cd->rhd", grad_scores, key_rows, preferred_element_type=jnp.float32)
        * score_scale
    )
    key_grad = (
        jnp.einsum("hrc,rhd->cd", grad_scores, query_rows, preferred_element_type=jnp.float32)
        * score_scale
    )
    value_grad = jnp.einsum("hrc,rhd->cd", probs_low, grad_rows, preferred_element_type=jnp.float32)
    return (query_grad, key_grad, value_grad)


def full_tile(operands):
    return tile_grads(
        operands[0],
        operands[1],
        operands[2],
        operands[3],
        operands[4],
        operands[5],
        operands[6],
        operands[7],
    )


def empty_grads(operands):
    query_rows = operands[0]
    key_rows = operands[5]
    return (
        jnp.zeros(query_rows.shape, jnp.float32),
        jnp.zeros(key_rows.shape, jnp.float32),
        jnp.zeros(key_rows.shape, jnp.float32),
    )


def sweep_keys(query_side, key_rows, value_rows):
    queries, grad_out, lse_rows, delta_rows, query_pos, own_starts, span_start = query_side
    row_count = queries.shape[0]
    span_rows = row_count // 2
    head_size = key_rows.shape[1]
    block_count = key_rows.shape[0] // row_count
    offsets = jnp.arange(span_rows, dtype=jnp.int32)
    query_init = jnp.zeros(queries.shape, jnp.float32)
    keys_init = jnp.zeros((key_rows.shape[0], 2 * head_size), jnp.float32)

    def sweep_turn(block_index, totals):
        query_total, key_total = totals
        key_block = lax.dynamic_slice_in_dim(key_rows, block_index * row_count, row_count, 0)
        value_block = lax.dynamic_slice_in_dim(value_rows, block_index * row_count, row_count, 0)
        block_starts = lax.dynamic_slice_in_dim(
            span_start, block_index * row_count // span_rows, 2, 0
        )
        query_parts = []
        key_parts = [
            jnp.zeros((span_rows, head_size), jnp.float32),
            jnp.zeros((span_rows, head_size), jnp.float32),
        ]
        value_parts = [
            jnp.zeros((span_rows, head_size), jnp.float32),
            jnp.zeros((span_rows, head_size), jnp.float32),
        ]
        for query_half in range(2):
            row_low = query_half * span_rows
            row_high = row_low + span_rows
            query_sum = jnp.zeros((span_rows,) + queries.shape[1:], jnp.float32)
            for key_half in range(2):
                key_low = key_half * span_rows
                key_high = key_low + span_rows
                operands = (
                    queries[row_low:row_high],
                    grad_out[row_low:row_high],
                    lse_rows[:, row_low:row_high],
                    delta_rows[:, row_low:row_high],
                    query_pos[row_low:row_high],
                    key_block[key_low:key_high],
                    value_block[key_low:key_high],
                    block_starts[key_half] + offsets,
                )
                tile_out = lax.cond(
                    block_starts[key_half] <= own_starts[query_half],
                    full_tile,
                    empty_grads,
                    operands,
                )
                query_sum = query_sum + tile_out[0]
                key_parts[key_half] = key_parts[key_half] + tile_out[1]
                value_parts[key_half] = value_parts[key_half] + tile_out[2]
            query_parts.append(query_sum)
        query_grad = jnp.concatenate(query_parts, axis=0)
        key_grad = jnp.concatenate(key_parts, axis=0)
        value_grad = jnp.concatenate(value_parts, axis=0)
        query_total = query_total + query_grad
        key_total = lax.dynamic_update_slice_in_dim(
            key_total, jnp.concatenate([key_grad, value_grad], axis=1), block_index * row_count, 0
        )
        return (query_total, key_total)

    return lax.fori_loop(0, block_count, sweep_turn, (query_init, keys_init))


def body(queries, keys, values, outputs, grad_held, lse, span_start):
    grad_next = from_behind(grad_held, "section", -1)
    query_block = queries[0]
    key_block = keys[0]
    value_block = values[0]
    row_count = query_block.shape[0]
    span_rows = row_count // 2
    head_size = key_block.shape[1]
    context = lax.axis_index("ctx")
    own_starts = lax.dynamic_slice_in_dim(span_start, 2 * context, 2, 0)
    offsets = jnp.arange(span_rows, dtype=jnp.int32)
    query_pos = (own_starts[:, None] + offsets[None, :]).reshape(row_count)
    grad_out = grad_next[0]
    delta_rows = jnp.sum(grad_out.astype(jnp.float32) * outputs[0].astype(jnp.float32), axis=-1).T
    query_side = (query_block, grad_out, lse[0], delta_rows, query_pos, own_starts, span_start)
    query_add, key_value_part = sweep_keys(
        query_side,
        lax.all_gather(key_block, "ctx", axis=0, tiled=True),
        lax.all_gather(value_block, "ctx", axis=0, tiled=True),
    )
    key_value_full = key_value_part
    query_total, key_value_full = (query_add, key_value_full)
    summed = lax.psum_scatter(
        key_value_full.astype(jnp.bfloat16), "ctx", scatter_dimension=0, tiled=True
    ).astype(jnp.float32)
    query_out = query_total.astype(jnp.bfloat16)[None]
    key_out = summed[:, :head_size].astype(jnp.bfloat16)[None]
    value_out = summed[:, head_size:].astype(jnp.bfloat16)[None]
    return (query_out, key_out, value_out)


def solution(mesh):
    placed = (
        P("section", "ctx", None, None),
        P("section", "ctx", None),
        P("section", "ctx", None),
        P("section", "ctx", None, None),
        P("section", "ctx", None, None),
        P("section", None, "ctx"),
        P(),
    )
    return jax.shard_map(
        body,
        mesh=mesh,
        in_specs=placed,
        out_specs=(
            P("section", "ctx", None, None),
            P("section", "ctx", None),
            P("section", "ctx", None),
        ),
        check_vma=False,
    )
```

profile of v0, /device:TPU:1, one launch (start us, length us, event | category | flops | bytes accessed | tf_op | source)
XLA Modules:
  0.0 633.8 jit_solution(2357705479401431310)
XLA Ops:
  8.7 2.6 copy.15
  11.3 7.4 %collective-permute-start = (bf16[1,256,16,128]{3,1,2,0:T(8,128)(2,1)}, bf16[1,256,16,128]{3,1,2,0:T(8,128)(2,1)S(1)}, u32[]{:S(2)}, u32[]{:S(2)}) collective-permute-start(bf16[1,256,16,128]{3,1,2,0:T(8,128)(2,1)} %copy.15), channel_id=1, source_target_pairs={{0,240},{16,0},{32,16},{48,32},{64,48},{80,64},{96,80},{112,96},{1... | collective-permute-start | bytes 3145736 | tf_op jit(solution)/shard_map/ppermute | solution.py:9
  22.3 19.4 %collective-permute-done = bf16[1,256,16,128]{3,1,2,0:T(8,128)(2,1)S(1)} collective-permute-done((bf16[1,256,16,128]{3,1,2,0:T(8,128)(2,1)}, bf16[1,256,16,128]{3,1,2,0:T(8,128)(2,1)S(1)}, u32[]{:S(2)}, u32[]{:S(2)}) %collective-permute-start) | collective-permute-done | bytes 1048608 | tf_op jit(solution)/shard_map/ppermute | solution.py:9
  42.4 39.9 %all-gather.5.cloned.1.call-done = bf16[1,4096,128]{2,1,0:T(8,128)(2,1)} async-done(((bf16[1,256,128]{2,1,0:T(8,128)(2,1)}), bf16[1,4096,128]{2,1,0:T(8,128)(2,1)}) %all-gather.5.cloned.1.call-update) | async-done | bytes 1048592 | tf_op jit(solution)/shard_map/all_gather | solution.py:144
  82.3 53.9 %all-gather.7.cloned.1.call-done = bf16[1,4096,128]{2,1,0:T(8,128)(2,1)} async-done(((bf16[1,256,128]{2,1,0:T(8,128)(2,1)}), bf16[1,4096,128]{2,1,0:T(8,128)(2,1)}) %all-gather.7.cloned.1.call-update) | async-done | bytes 1048592 | tf_op jit(solution)/shard_map/all_gather | solution.py:145
  137.7 401.6 %while.19 = (s32[]{:T(128)}, f32[256,16,128]{2,0,1:T(8,128)}, bf16[4096,256]{1,0:T(8,128)(2,1)}, s32[32]{0:T(128)}, s32[2]{0:T(128)}, /*index=5*/bf16[4096,128]{...) while((s32[]{:T(128)}, f32[256,16,128]{2,0,1:T(8,128)}, ...), condition=%wide.region_10.11_spmd.clone.clone, body=%wide.region_1.10_spmd.clone.clone.sunk | while | flops 1353384192 | bytes 84388064 | solution.py:124
  146.8 2.0 fusion.94
  153.7 2.4 conditional.16
  156.1 2.4 conditional.17
  172.2 2.0 fusion.94
  180.7 2.4 conditional.16
  183.1 2.4 conditional.17
  199.2 2.0 fusion.94
  207.7 2.4 conditional.16
  224.0 2.0 fusion.94
  230.9 2.4 conditional.16
  233.3 2.4 conditional.17
  249.4 2.0 fusion.94
  257.8 2.4 conditional.16
  274.1 2.0 fusion.94
  278.3 1.7 conditional.18
  282.6 2.4 conditional.16
  298.9 2.0 fusion.94
  307.3 2.4 conditional.16
  323.7 2.0 fusion.94
  332.1 2.4 conditional.16
  348.4 2.0 fusion.94
  356.9 2.4 conditional.16
  373.2 2.0 fusion.94
  377.3 1.7 conditional.18
  381.6 2.4 conditional.16
  397.9 2.0 fusion.94
  404.8 2.4 conditional.16
  407.2 2.4 conditional.17
  423.4 2.0 fusion.94
  430.3 2.4 conditional.16
  432.7 2.4 conditional.17
  448.8 2.0 fusion.94
  457.2 2.4 conditional.16
  473.6 2.0 fusion.94
  482.0 2.4 conditional.16
  498.3 2.0 fusion.94
  505.2 2.4 conditional.16
  507.6 2.4 conditional.17
  523.7 2.0 fusion.94
  532.2 2.4 conditional.16
  540.9 2.2 copy.27
  543.1 82.6 %reduce-scatter.2.cloned.1.call-done = bf16[256,256]{1,0:T(8,128)(2,1)} async-done(((bf16[4096,256]{1,0:T(8,128)(2,1)}), bf16[256,256]{1,0:T(8,128)(2,1)}) %reduce-scatter.2.cloned.1.call-update) | async-done | bytes 131088 | tf_op jit(solution)/shard_map/reduce_scatter | solution.py:149
  (912 shorter events, 309.0 us)
Async XLA Ops:
  7.2 11.5 %copy-start.8 = (bf16[1,256,16,128]{3,2,1,0:T(8,128)(2,1)S(1)}, bf16[1,256,16,128]{3,2,1,0:T(8,128)(2,1)}, u32[]{:S(2)}) copy-start(bf16[1,256,16,128]{3,2,1,0:T(8,128)(2,1)} %param.17) | copy-start | bytes 3145732
  7.2 75.1 %all-gather.5.cloned.1.call-start = ((), (), s32[]{:S(2)}) async-start(), calls=%async_computation.2 | async-start | bytes 1114112 | tf_op jit(solution)/shard_map/all_gather | solution.py:144
  7.9 128.3 %all-gather.7.cloned.1.call-start = ((), (), s32[]{:S(2)}) async-start(), calls=%async_computation.3 | async-start | bytes 1114112 | tf_op jit(solution)/shard_map/all_gather | solution.py:145
  8.7 33.0 %copy-start.9 = (bf16[1,256,16,128]{3,2,1,0:T(8,128)(2,1)S(1)}, bf16[1,256,16,128]{3,2,1,0:T(8,128)(2,1)}, u32[]{:S(2)}) copy-start(bf16[1,256,16,128]{3,2,1,0:T(8,128)(2,1)} %param.20) | copy-start | bytes 3145732
  8.7 617.0 %reduce-scatter.2.cloned.1.call-start = ((), (), s32[]{:S(2)}) async-start(), calls=%async_computation.1 | async-start | bytes 2228224 | tf_op jit(solution)/shard_map/reduce_scatter | solution.py:149
  11.3 30.4 %collective-permute-start = (bf16[1,256,16,128]{3,1,2,0:T(8,128)(2,1)}, bf16[1,256,16,128]{3,1,2,0:T(8,128)(2,1)S(1)}, u32[]{:S(2)}, u32[]{:S(2)}) collective-permute-start(bf16[1,256,16,128]{3,1,2,0:T(8,128)(2,1)} %copy.15), channel_id=1, source_target_pairs={{0,240},{16,0},{32,16},{48,32},{64,48},{80,64},{96,80},{112,96},{1... | collective-permute-start | bytes 3145736 | tf_op jit(solution)/shard_map/ppermute | solution.py:9
  22.3 115.4 %copy-start.12 = (f32[1,16,256]{2,1,0:T(8,128)S(1)}, f32[1,16,256]{2,1,0:T(8,128)}, u32[]{:S(2)}) copy-start(f32[1,16,256]{2,1,0:T(8,128)} %param.22) | copy-start | bytes 49156
  137.7 13.2 %copy-start.5 = (bf16[256,16,128]{2,0,1:T(8,128)(2,1)}, bf16[256,16,128]{2,0,1:T(8,128)(2,1)S(1)}, u32[]{:S(2)}) copy-start(bf16[256,16,128]{2,0,1:T(8,128)(2,1)S(1)} %get-tuple-element.783) | copy-start | bytes 3145732 | tf_op jit(solution)/shard_map/while
  137.7 13.2 %copy-start.10 = (f32[16,256]{1,0:T(8,128)}, f32[16,256]{1,0:T(8,128)S(1)}, u32[]{:S(2)}) copy-start(f32[16,256]{1,0:T(8,128)S(1)} %get-tuple-element.784) | copy-start | bytes 49156 | tf_op jit(solution)/shard_map/while
  158.5 2.4 copy-start.2
  163.1 13.3 %copy-start.5 = (bf16[256,16,128]{2,0,1:T(8,128)(2,1)}, bf16[256,16,128]{2,0,1:T(8,128)(2,1)S(1)}, u32[]{:S(2)}) copy-start(bf16[256,16,128]{2,0,1:T(8,128)(2,1)S(1)} %get-tuple-element.783) | copy-start | bytes 3145732 | tf_op jit(solution)/shard_map/while
  163.1 13.3 %copy-start.10 = (f32[16,256]{1,0:T(8,128)}, f32[16,256]{1,0:T(8,128)S(1)}, u32[]{:S(2)}) copy-start(f32[16,256]{1,0:T(8,128)S(1)} %get-tuple-element.784) | copy-start | bytes 49156 | tf_op jit(solution)/shard_map/while
  185.5 2.4 copy-start.2
  190.0 13.3 %copy-start.5 = (bf16[256,16,128]{2,0,1:T(8,128)(2,1)}, bf16[256,16,128]{2,0,1:T(8,128)(2,1)S(1)}, u32[]{:S(2)}) copy-start(bf16[256,16,128]{2,0,1:T(8,128)(2,1)S(1)} %get-tuple-element.783) | copy-start | bytes 3145732 | tf_op jit(solution)/shard_map/while
  190.0 13.3 %copy-start.10 = (f32[16,256]{1,0:T(8,128)}, f32[16,256]{1,0:T(8,128)S(1)}, u32[]{:S(2)}) copy-start(f32[16,256]{1,0:T(8,128)S(1)} %get-tuple-element.784) | copy-start | bytes 49156 | tf_op jit(solution)/shard_map/while
  210.2 2.4 copy-start.2
  214.8 13.3 %copy-start.5 = (bf16[256,16,128]{2,0,1:T(8,128)(2,1)}, bf16[256,16,128]{2,0,1:T(8,128)(2,1)S(1)}, u32[]{:S(2)}) copy-start(bf16[256,16,128]{2,0,1:T(8,128)(2,1)S(1)} %get-tuple-element.783) | copy-start | bytes 3145732 | tf_op jit(solution)/shard_map/while
  214.8 13.3 %copy-start.10 = (f32[16,256]{1,0:T(8,128)}, f32[16,256]{1,0:T(8,128)S(1)}, u32[]{:S(2)}) copy-start(f32[16,256]{1,0:T(8,128)S(1)} %get-tuple-element.784) | copy-start | bytes 49156 | tf_op jit(solution)/shard_map/while
  235.7 2.4 copy-start.2
  240.2 13.3 %copy-start.5 = (bf16[256,16,128]{2,0,1:T(8,128)(2,1)}, bf16[256,16,128]{2,0,1:T(8,128)(2,1)S(1)}, u32[]{:S(2)}) copy-start(bf16[256,16,128]{2,0,1:T(8,128)(2,1)S(1)} %get-tuple-element.783) | copy-start | bytes 3145732 | tf_op jit(solution)/shard_map/while
  240.2 13.3 %copy-start.10 = (f32[16,256]{1,0:T(8,128)}, f32[16,256]{1,0:T(8,128)S(1)}, u32[]{:S(2)}) copy-start(f32[16,256]{1,0:T(8,128)S(1)} %get-tuple-element.784) | copy-start | bytes 49156 | tf_op jit(solution)/shard_map/while
  260.4 2.4 copy-start.2
  265.0 13.3 %copy-start.5 = (bf16[256,16,128]{2,0,1:T(8,128)(2,1)}, bf16[256,16,128]{2,0,1:T(8,128)(2,1)S(1)}, u32[]{:S(2)}) copy-start(bf16[256,16,128]{2,0,1:T(8,128)(2,1)S(1)} %get-tuple-element.783) | copy-start | bytes 3145732 | tf_op jit(solution)/shard_map/while
  265.0 13.3 %copy-start.10 = (f32[16,256]{1,0:T(8,128)}, f32[16,256]{1,0:T(8,128)S(1)}, u32[]{:S(2)}) copy-start(f32[16,256]{1,0:T(8,128)S(1)} %get-tuple-element.784) | copy-start | bytes 49156 | tf_op jit(solution)/shard_map/while
  285.2 2.4 copy-start.2
  289.7 13.3 %copy-start.5 = (bf16[256,16,128]{2,0,1:T(8,128)(2,1)}, bf16[256,16,128]{2,0,1:T(8,128)(2,1)S(1)}, u32[]{:S(2)}) copy-start(bf16[256,16,128]{2,0,1:T(8,128)(2,1)S(1)} %get-tuple-element.783) | copy-start | bytes 3145732 | tf_op jit(solution)/shard_map/while
  289.7 13.3 %copy-start.10 = (f32[16,256]{1,0:T(8,128)}, f32[16,256]{1,0:T(8,128)S(1)}, u32[]{:S(2)}) copy-start(f32[16,256]{1,0:T(8,128)S(1)} %get-tuple-element.784) | copy-start | bytes 49156 | tf_op jit(solution)/shard_map/while
  309.9 2.4 copy-start.2
  314.5 13.3 %copy-start.5 = (bf16[256,16,128]{2,0,1:T(8,128)(2,1)}, bf16[256,16,128]{2,0,1:T(8,128)(2,1)S(1)}, u32[]{:S(2)}) copy-start(bf16[256,16,128]{2,0,1:T(8,128)(2,1)S(1)} %get-tuple-element.783) | copy-start | bytes 3145732 | tf_op jit(solution)/shard_map/while
  314.5 13.3 %copy-start.10 = (f32[16,256]{1,0:T(8,128)}, f32[16,256]{1,0:T(8,128)S(1)}, u32[]{:S(2)}) copy-start(f32[16,256]{1,0:T(8,128)S(1)} %get-tuple-element.784) | copy-start | bytes 49156 | tf_op jit(solution)/shard_map/while
  339.2 13.3 %copy-start.5 = (bf16[256,16,128]{2,0,1:T(8,128)(2,1)}, bf16[256,16,128]{2,0,1:T(8,128)(2,1)S(1)}, u32[]{:S(2)}) copy-start(bf16[256,16,128]{2,0,1:T(8,128)(2,1)S(1)} %get-tuple-element.783) | copy-start | bytes 3145732 | tf_op jit(solution)/shard_map/while
  339.3 13.3 %copy-start.10 = (f32[16,256]{1,0:T(8,128)}, f32[16,256]{1,0:T(8,128)S(1)}, u32[]{:S(2)}) copy-start(f32[16,256]{1,0:T(8,128)S(1)} %get-tuple-element.784) | copy-start | bytes 49156 | tf_op jit(solution)/shard_map/while
  359.4 2.4 copy-start.2
  364.0 13.3 %copy-start.5 = (bf16[256,16,128]{2,0,1:T(8,128)(2,1)}, bf16[256,16,128]{2,0,1:T(8,128)(2,1)S(1)}, u32[]{:S(2)}) copy-start(bf16[256,16,128]{2,0,1:T(8,128)(2,1)S(1)} %get-tuple-element.783) | copy-start | bytes 3145732 | tf_op jit(solution)/shard_map/while
  364.0 13.3 %copy-start.10 = (f32[16,256]{1,0:T(8,128)}, f32[16,256]{1,0:T(8,128)S(1)}, u32[]{:S(2)}) copy-start(f32[16,256]{1,0:T(8,128)S(1)} %get-tuple-element.784) | copy-start | bytes 49156 | tf_op jit(solution)/shard_map/while
  388.8 13.3 %copy-start.5 = (bf16[256,16,128]{2,0,1:T(8,128)(2,1)}, bf16[256,16,128]{2,0,1:T(8,128)(2,1)S(1)}, u32[]{:S(2)}) copy-start(bf16[256,16,128]{2,0,1:T(8,128)(2,1)S(1)} %get-tuple-element.783) | copy-start | bytes 3145732 | tf_op jit(solution)/shard_map/while
  388.8 13.3 %copy-start.10 = (f32[16,256]{1,0:T(8,128)}, f32[16,256]{1,0:T(8,128)S(1)}, u32[]{:S(2)}) copy-start(f32[16,256]{1,0:T(8,128)S(1)} %get-tuple-element.784) | copy-start | bytes 49156 | tf_op jit(solution)/shard_map/while
  414.2 13.3 %copy-start.5 = (bf16[256,16,128]{2,0,1:T(8,128)(2,1)}, bf16[256,16,128]{2,0,1:T(8,128)(2,1)S(1)}, u32[]{:S(2)}) copy-start(bf16[256,16,128]{2,0,1:T(8,128)(2,1)S(1)} %get-tuple-element.783) | copy-start | bytes 3145732 | tf_op jit(solution)/shard_map/while
  414.2 13.3 %copy-start.10 = (f32[16,256]{1,0:T(8,128)}, f32[16,256]{1,0:T(8,128)S(1)}, u32[]{:S(2)}) copy-start(f32[16,256]{1,0:T(8,128)S(1)} %get-tuple-element.784) | copy-start | bytes 49156 | tf_op jit(solution)/shard_map/while
  435.1 2.4 copy-start.2
  439.6 13.3 %copy-start.5 = (bf16[256,16,128]{2,0,1:T(8,128)(2,1)}, bf16[256,16,128]{2,0,1:T(8,128)(2,1)S(1)}, u32[]{:S(2)}) copy-start(bf16[256,16,128]{2,0,1:T(8,128)(2,1)S(1)} %get-tuple-element.783) | copy-start | bytes 3145732 | tf_op jit(solution)/shard_map/while
  439.6 13.3 %copy-start.10 = (f32[16,256]{1,0:T(8,128)}, f32[16,256]{1,0:T(8,128)S(1)}, u32[]{:S(2)}) copy-start(f32[16,256]{1,0:T(8,128)S(1)} %get-tuple-element.784) | copy-start | bytes 49156 | tf_op jit(solution)/shard_map/while
  464.4 13.3 %copy-start.5 = (bf16[256,16,128]{2,0,1:T(8,128)(2,1)}, bf16[256,16,128]{2,0,1:T(8,128)(2,1)S(1)}, u32[]{:S(2)}) copy-start(bf16[256,16,128]{2,0,1:T(8,128)(2,1)S(1)} %get-tuple-element.783) | copy-start | bytes 3145732 | tf_op jit(solution)/shard_map/while
  464.4 13.3 %copy-start.10 = (f32[16,256]{1,0:T(8,128)}, f32[16,256]{1,0:T(8,128)S(1)}, u32[]{:S(2)}) copy-start(f32[16,256]{1,0:T(8,128)S(1)} %get-tuple-element.784) | copy-start | bytes 49156 | tf_op jit(solution)/shard_map/while
  489.2 13.3 %copy-start.5 = (bf16[256,16,128]{2,0,1:T(8,128)(2,1)}, bf16[256,16,128]{2,0,1:T(8,128)(2,1)S(1)}, u32[]{:S(2)}) copy-start(bf16[256,16,128]{2,0,1:T(8,128)(2,1)S(1)} %get-tuple-element.783) | copy-start | bytes 3145732 | tf_op jit(solution)/shard_map/while
  489.2 13.3 %copy-start.10 = (f32[16,256]{1,0:T(8,128)}, f32[16,256]{1,0:T(8,128)S(1)}, u32[]{:S(2)}) copy-start(f32[16,256]{1,0:T(8,128)S(1)} %get-tuple-element.784) | copy-start | bytes 49156 | tf_op jit(solution)/shard_map/while
  514.6 13.3 %copy-start.5 = (bf16[256,16,128]{2,0,1:T(8,128)(2,1)}, bf16[256,16,128]{2,0,1:T(8,128)(2,1)S(1)}, u32[]{:S(2)}) copy-start(bf16[256,16,128]{2,0,1:T(8,128)(2,1)S(1)} %get-tuple-element.783) | copy-start | bytes 3145732 | tf_op jit(solution)/shard_map/while
  514.6 13.3 %copy-start.10 = (f32[16,256]{1,0:T(8,128)}, f32[16,256]{1,0:T(8,128)S(1)}, u32[]{:S(2)}) copy-start(f32[16,256]{1,0:T(8,128)S(1)} %get-tuple-element.784) | copy-start | bytes 49156 | tf_op jit(solution)/shard_map/while
  (120 other events, 211.6 us)
Sparse Core Ops, SparseCore 0:
  10.7 71.5 all-gather.4
  85.0 51.1 all-gather.6
  539.5 86.1 reduce-scatter.1
where the time goes:
time: 640 us; the launch traced here: 634 us
  waiting for transfers between devices  197 us (31%)
  local copies, waits for them, and re-layouts  137 us (21%)
  other arithmetic  136 us (21%)
  loops' own time  91.4 us (14%)
  matrix products  51.3 us (8%)
  between operations  13.8 us (2%)
  starting transfers between devices  7.47 us (1%)
    another operation x1, loops' own time, sweep_keys(): return lax.fori_loop(0, block_count, sweep_turn, (query_init, keys_init))  88.3 us
    reduce_scatter x1, waiting for transfers between devices, body(): lax.psum_scatter(key_value_full.astype(jnp.bfloat16), 'ctx', scatter_dime...  82.6 us
    all_gather x1, waiting for transfers between devices, body(): lax.all_gather(value_block, 'ctx', axis=0, tiled=True)  53.9 us
    while x320, local copies, waits for them, and re-layouts  44.6 us
    add x32, other arithmetic, sweep_turn(): query_sum = query_sum + tile_out[0]  42.8 us
    all_gather x1, waiting for transfers between devices, body(): lax.all_gather(key_block, 'ctx', axis=0, tiled=True)  39.9 us
    slice x16, other arithmetic, sweep_turn(): query_pos[row_low:row_high]  31.5 us
    slice x16, local copies, waits for them, and re-layouts, sweep_turn(): grad_out[row_low:row_high]  21.6 us
  transfers between devices with their start and end apart: 4, of which 4 were waited for; matrix products, arithmetic and copies ran while one was open for 1% of the time, Pallas kernels for 0%

commit v1 on v0

v1 whole, which is shorter than its diff:
```python
import jax
import jax.numpy as jnp
from jax import lax
from jax.experimental import pallas as pl
from jax.experimental.pallas import tpu as pltpu
from jax.sharding import PartitionSpec as P

bf16, f32 = jnp.bfloat16, jnp.float32
LOG2E = 1.4426950408889634
FAR = 1e30
MESH = pl.DeviceIdType.MESH
PHASES = 2


def nn(a, b):
    return lax.dot_general(a, b, (((1,), (0,)), ((), ())), preferred_element_type=f32)


def nt(a, b):
    return lax.dot_general(a, b, (((1,), (1,)), ((), ())), preferred_element_type=f32)


def pair(top_left, top_right, bottom_left, bottom_right):
    top = jnp.concatenate([top_left, top_right], 1)
    return jnp.concatenate([top, jnp.concatenate([bottom_left, bottom_right], 1)], 0)


def attend(key_pair, value_pair, lse_pair, delta_pair, mask, rows, qc, dc, dq):
    span = key_pair.shape[0] // 2
    scale2 = (key_pair.shape[1] // 2) ** -0.5 * LOG2E
    scores = nt(key_pair, qc[rows, :]) * scale2
    grads = nt(value_pair, dc[rows, :])
    probs, terms = [], []
    for slot in range(2):
        part = slice(slot * span, (slot + 1) * span)
        prob = jnp.exp2(scores[part] - lse_pair[slot])
        if mask is not None:
            prob = jnp.where(mask, prob, 0.0)
        probs.append(prob)
        terms.append(prob * (grads[part] - delta_pair[slot]))
    probs = jnp.concatenate(probs, 0).astype(bf16)
    terms = jnp.concatenate(terms, 0).astype(bf16)
    dq[:, rows] += nn(key_pair.T, terms)
    return nn(terms, qc[rows, :]), nn(probs, dc[rows, :])


def kernel(
    starts, q, k, v, g, o, lse, dq_out, dk_out, dv_out,
    qc, dc, ob, lb, kv, dq, lse_rows, delta, acc, cred, send1, send2, yred, zsend, zred,
    in_s, grad_s, grad_r, kv_s, kv_r, fwd_s, s1_s, s1_r, s2_s, s2_r, z_s, z_r,
):
    me, sec = lax.axis_index("ctx"), lax.axis_index("section")
    sections = lax.axis_size("section")
    half_rows, head = qc.shape[0], qc.shape[1] // 2
    span = kv.shape[1] // 2
    scale = head ** -0.5
    step = half_rows // PHASES
    zh, y, core = me // 8, (me // 2) % 4, me % 2

    def at(dz, dy, dc):
        return (((zh + dz) % 2) * 4 + (y + dy) % 4) * 2 + (core + dc) % 2

    def index_of(j):
        return at(j // 8, j % 4, (j // 4) % 2)

    def remote(src, dst, send, recv, target):
        return pltpu.make_async_remote_copy(
            src_ref=src, dst_ref=dst, send_sem=send, recv_sem=recv,
            device_id=target, device_id_type=MESH,
        )

    core_peer, z_peer = {"ctx": at(0, 0, 1)}, {"ctx": at(1, 0, 0)}
    y_peers = [{"ctx": at(0, dy, 0)} for dy in (1, 2, 3)]
    before = {"section": (sec + sections - 1) % sections}
    after = {"section": (sec + 1) % sections}

    local = [
        pltpu.make_async_copy(k, kv.at[me, :, pl.ds(0, head)], in_s.at[0]),
        pltpu.make_async_copy(v, kv.at[me, :, pl.ds(head, head)], in_s.at[1]),
        pltpu.make_async_copy(lse, lb, in_s.at[2]),
    ]
    for half in range(2):
        part, cols = pl.ds(half * half_rows, half_rows), pl.ds(half * head, head)
        local.append(pltpu.make_async_copy(q.at[part, :], qc.at[:, cols], in_s.at[3 + half]))
        local.append(pltpu.make_async_copy(o.at[part, :], ob.at[:, cols], in_s.at[5 + half]))
    for copy in local:
        copy.start()

    barrier = pltpu.get_barrier_semaphore()
    peers = [core_peer, z_peer, *y_peers, before, after]
    for peer in peers:
        pl.semaphore_signal(barrier, inc=1, device_id=peer, device_id_type=MESH)
    pl.semaphore_wait(barrier, len(peers))

    grads = []
    for phase in range(PHASES):
        for half in range(2):
            n = phase * 2 + half
            grads.append(
                remote(
                    g.at[pl.ds(half * half_rows + phase * step, step), :],
                    dc.at[pl.ds(phase * step, step), pl.ds(half * head, head)],
                    grad_s.at[n], grad_r.at[n], before,
                )
            )
            grads[-1].start()
    for copy in local[:2]:
        copy.wait()

    def spread(shard, base, first):
        out = []
        for n, (peer, slot) in enumerate(
            [(y_peers[0], 3), (y_peers[2], 1), (y_peers[1], 2), (core_peer, 4)]
        ):
            out.append(
                remote(kv.at[shard], kv.at[shard], kv_s.at[base + n], kv_r.at[first + slot], peer)
            )
            out[-1].start()
        return out

    def arrived(j):
        spot = kv.at[index_of(j)]
        remote(spot, spot, kv_s.at[0], kv_r.at[j], core_peer).wait_recv()

    def forward(j):
        spot = kv.at[index_of(j)]
        return remote(spot, spot, fwd_s.at[j], kv_r.at[j + 4], core_peer)

    z_copy = remote(kv.at[me], kv.at[me], kv_s.at[8], kv_r.at[8], z_peer)
    z_copy.start()
    kv_copies = [z_copy, *spread(me, 0, 0)]

    dq[...] = jnp.zeros_like(dq)
    for copy in local[2:]:
        copy.wait()
    lane = lax.broadcasted_iota(jnp.int32, (16, 128), 1)
    pick = jnp.where(lane % 16 == lax.broadcasted_iota(jnp.int32, (16, 128), 0), 1.0, 0.0).astype(f32)
    tokens = lax.broadcasted_iota(jnp.int32, (128, 128), 0)
    lanes = lax.broadcasted_iota(jnp.int32, (128, 128), 1)
    for half in range(2):
        part = lb[:, half * 128 : (half + 1) * 128] * LOG2E
        wide = lax.dot_general(
            part, pick, (((0,), (0,)), ((), ())),
            precision=lax.Precision.HIGHEST, preferred_element_type=f32,
        )
        wide = jnp.where(lanes // 16 == tokens % 8, wide, 0.0)
        packed = jnp.sum(wide.reshape(16, 8, 128), axis=1)
        for i in range(16):
            lse_rows[half, :, i * 128 : (i + 1) * 128] = packed[i : i + 1]

    for j in (1, 3, 2):
        arrived(j)
        forward(j).start()
    arrived(8)
    kv_copies += spread(index_of(8), 4, 8)

    zero = jnp.zeros((span, head), bf16)
    low_start = starts[2 * me]
    ones = jnp.ones((8, head), bf16)

    def rows_of(phase):
        return pl.ds(phase * step, step)

    def start_phase(phase):
        rows = rows_of(phase)
        for half in range(2):
            grads[phase * 2 + half].wait_recv()
        for half in range(2):
            cols = pl.ds(half * head, head)
            prod = dc[rows, cols].astype(f32) * ob[rows, cols].astype(f32)
            high = prod.astype(bf16)
            low = (prod - high.astype(f32)).astype(bf16)
            delta[half, :, rows] = (nt(ones, high) + nt(ones, low))[:1]

    def diagonal(phase):
        rows = rows_of(phase)
        token = lax.shift_right_logical(
            lax.broadcasted_iota(jnp.int32, (span, step), 1), (half_rows // span).bit_length() - 1
        ) + phase * (step * span // half_rows)
        mask = lax.broadcasted_iota(jnp.int32, (span, step), 0) <= token
        k_a, k_b = kv[me, :span, :head], kv[me, span:, :head]
        v_a, v_b = kv[me, :span, head:], kv[me, span:, head:]
        dk, dv = attend(
            pair(zero, k_b, k_a, zero),
            pair(zero, v_b, v_a, zero),
            (lse_rows[1, :, rows], lse_rows[0, :, rows]),
            (delta[1, :, rows], delta[0, :, rows]),
            mask, rows, qc, dc, dq,
        )
        dk *= scale
        return pair(dk[span:, :head], dv[span:, :head], dk[:span, head:], dv[:span, head:])

    def shard_terms(j, phase):
        rows = rows_of(phase)
        m = index_of(j)
        sel = starts[2 * m] < low_start
        on = jnp.where(sel, 1.0, 0.0).astype(f32)
        off = 1.0 - on
        lse_a, lse_b = lse_rows[0, :, rows], lse_rows[1, :, rows]
        del_a, del_b = delta[0, :, rows], delta[1, :, rows]
        k_a, k_b = kv[m, :span, :head], kv[m, span:, :head]
        v_a, v_b = kv[m, :span, head:], kv[m, span:, head:]
        dk, dv = attend(
            pair(zero, k_a, (k_a * on).astype(bf16), (k_b * off).astype(bf16)),
            pair(zero, v_a, (v_a * on).astype(bf16), (v_b * off).astype(bf16)),
            (lse_b, jnp.where(j == 0, FAR, jnp.where(sel, lse_a, lse_b))),
            (del_b, jnp.where(sel, del_a, del_b)),
            None, rows, qc, dc, dq,
        )
        dk *= scale
        return pair(
            dk[:span, head:] + on * dk[span:, :head],
            dv[:span, head:] + on * dv[span:, :head],
            off * dk[span:, head:],
            off * dv[span:, head:],
        )

    def finish_rows(phase):
        for half in range(2):
            part = dq[half * head : (half + 1) * head, phase * step : (phase + 1) * step]
            dq_out[pl.ds(half * half_rows + phase * step, step), :] = (part.T * scale).astype(bf16)

    start_phase(0)
    acc[0] = diagonal(0)

    def first(j, carry):
        waits = jnp.logical_or(j // 4 == 1, j >= 9)

        @pl.when(waits)
        def _():
            arrived(j)

        @pl.when(jnp.logical_and(j >= 9, j < 12))
        def _():
            forward(j).start()

        terms = shard_terms(j, 0)

        @pl.when(j == 0)
        def _():
            acc[0] += terms

        @pl.when(j > 0)
        def _():
            acc[j] = terms

        return carry

    lax.fori_loop(0, 16, first, 0)
    finish_rows(0)
    start_phase(1)

    def sum1(n):
        return remote(send1.at[n], cred.at[n], s1_s.at[n], s1_r.at[n], core_peer)

    def sum2(n):
        dy = n % 4
        back = (n // 4) * 4 + (4 - dy) % 4
        return remote(
            send2.at[n], yred.at[back], s2_s.at[n], s2_r.at[back], {"ctx": at(0, dy, 0)}
        )

    def got2(n):
        remote(send2.at[n], yred.at[n], s2_s.at[n], s2_r.at[n], core_peer).wait_recv()

    z_sum = remote(zsend, zred, z_s.at[0], z_r.at[0], z_peer)

    def second(i, carry):
        j = 15 - i
        n = (j // 8) * 4 + j % 4
        terms = acc[j] + shard_terms(j, 1)
        kept = (j // 4) % 2 == 0

        @pl.when(jnp.logical_not(kept))
        def _():
            send1[n] = terms.astype(bf16)
            sum1(n).start()

        @pl.when(kept)
        def _():
            sum1(n).wait_recv()
            total = terms + cred[n].astype(f32)

            @pl.when(j % 4 == 0)
            def _():
                acc[j] = total

            @pl.when(j % 4 != 0)
            def _():
                send2[n] = total.astype(bf16)
                sum2(n).start()

        @pl.when(j == 5)
        def _():
            total = acc[8]
            for dy in (1, 2, 3):
                got2(4 + dy)
                total += yred[4 + dy].astype(f32)
            zsend[...] = total.astype(bf16)
            z_sum.start()

        return carry

    lax.fori_loop(0, 16, second, 0)
    total = acc[0] + diagonal(1)
    finish_rows(1)
    for dy in (1, 2, 3):
        got2(dy)
        total += yred[dy].astype(f32)
    z_sum.wait_recv()
    total += zred[...].astype(f32)
    dk_out[...] = total[:, :head].astype(bf16)
    dv_out[...] = total[:, head:].astype(bf16)

    for copy in grads + kv_copies:
        copy.wait_send()
    for j in (1, 2, 3, 9, 10, 11):
        forward(j).wait_send()
    for n in range(8):
        sum1(n).wait_send()
        if n % 4:
            sum2(n).wait_send()
    z_sum.wait_send()


def body(queries, keys, values, outputs, grad_held, lse, span_start):
    tokens, heads, head = queries.shape[1:]
    n = lax.axis_size("ctx")
    rows = tokens * heads // 2
    vm = pl.BlockSpec(memory_space=pltpu.VMEM)
    hbm = pl.BlockSpec(memory_space=pl.ANY)
    dma = pltpu.SemaphoreType.DMA
    tile = (tokens, 2 * head)
    dq, dk, dv = pl.pallas_call(
        kernel,
        out_shape=(
            jax.ShapeDtypeStruct((2 * rows, head), bf16),
            jax.ShapeDtypeStruct((tokens, head), bf16),
            jax.ShapeDtypeStruct((tokens, head), bf16),
        ),
        in_specs=[pl.BlockSpec(memory_space=pltpu.SMEM)] + [hbm] * 6,
        out_specs=(vm, vm, vm),
        scratch_shapes=[
            pltpu.VMEM((rows, 2 * head), bf16),
            pltpu.VMEM((rows, 2 * head), bf16),
            pltpu.VMEM((rows, 2 * head), bf16),
            pltpu.VMEM((heads, tokens), f32),
            pltpu.VMEM((n, *tile), bf16),
            pltpu.VMEM((2 * head, rows), f32),
            pltpu.VMEM((2, 1, rows), f32),
            pltpu.VMEM((2, 1, rows), f32),
            pltpu.VMEM((n, *tile), f32),
            pltpu.VMEM((8, *tile), bf16),
            pltpu.VMEM((8, *tile), bf16),
            pltpu.VMEM((8, *tile), bf16),
            pltpu.VMEM((8, *tile), bf16),
            pltpu.VMEM(tile, bf16),
            pltpu.VMEM(tile, bf16),
            dma((7,)), dma((4,)), dma((4,)), dma((9,)), dma((16,)), dma((12,)),
            dma((8,)), dma((8,)), dma((8,)), dma((8,)), dma((1,)), dma((1,)),
        ],
        compiler_params=pltpu.CompilerParams(
            vmem_limit_bytes=60 << 20, collective_id=0, has_side_effects=True
        ),
    )(
        span_start,
        queries.reshape(2 * rows, head),
        keys[0],
        values[0],
        grad_held.reshape(2 * rows, head),
        outputs.reshape(2 * rows, head),
        lse[0],
    )
    return dq.reshape(1, tokens, heads, head), dk[None], dv[None]


def solution(mesh):
    rows = P("section", "ctx", None, None)
    keys = P("section", "ctx", None)
    return jax.shard_map(
        body,
        mesh=mesh,
        in_specs=(rows, keys, keys, rows, rows, P("section", None, "ctx"), P()),
        out_specs=(rows, keys, keys),
        check_vma=False,
    )
```

time: 640 us -> 92.7 us (0.14)
  waiting for transfers between devices: 197 us -> 0 us
  other arithmetic: 136 us -> 0 us
  local copies, waits for them, and re-layouts: 137 us -> 3.9 us
  loops' own time: 91.4 us -> 0 us
  Pallas kernels: 0 us -> 87.9 us
  matrix products: 51.3 us -> 0 us
  between operations: 13.8 us -> 0.65 us
  starting transfers between devices: 7.47 us -> 0 us
    all_gather x2 -> x0, waiting for transfers between devices: 93.9 us -> none  [the longest x1 53.9 us: body(): lax.all_gather(value_block, 'ctx', axis=0, tiled=True)]
    another operation x65 -> x0, loops' own time: 91.4 us -> none  [the longest x1 88.3 us: sweep_keys(): return lax.fori_loop(0, block_count, sweep_turn, (query_init, keys_init))]
    pallas_call x0 -> x1, Pallas kernels: none -> 87.9 us  [body(): pl.pallas_call(kernel, out_shape=(jax.ShapeDtypeStruct((2 * rows, head),...]
    reduce_scatter x1 -> x0, waiting for transfers between devices: 82.6 us -> none  [body(): lax.psum_scatter(key_value_full.astype(jnp.bfloat16), 'ctx', scatter_dime...]
    add x129 -> x0, other arithmetic: 74.1 us -> none  [the longest x32 42.8 us: sweep_turn(): query_sum = query_sum + tile_out[0]]
    slice x80 -> x0, local copies, waits for them, and re-layouts: 65 us -> none  [the longest x16 21.6 us: sweep_turn(): grad_out[row_low:row_high]]
    dot_general x165 -> x0, matrix products: 51.3 us -> none  [the longest x33 11.7 us: tile_grads(): jnp.einsum('rhd,cd->hrc', query_rows, key_rows, preferred_element_type=jn...]
    while x321 -> x0, local copies, waits for them, and re-layouts: 46.8 us -> none
  transfers between devices with their start and end apart: 4 -> 0, of which waited for: 4 -> 0; matrix products, arithmetic and copies ran while one was open for 1% -> 0% of each run, Pallas kernels for 0% -> 0%
where the time goes in v1:
time: 92.7 us; the launch traced here: 92.5 us
  Pallas kernels  87.9 us (95%)
  local copies, waits for them, and re-layouts  3.9 us (4%)
    pallas_call x1, Pallas kernels, body(): pl.pallas_call(kernel, out_shape=(jax.ShapeDtypeStruct((2 * rows, head),...  87.9 us
    unnamed x7, local copies, waits for them, and re-layouts  3.9 us

profile of v1, /device:TPU:1, one launch (start us, length us, event | category | flops | bytes accessed | tf_op | source)
XLA Modules:
  0.0 92.5 jit_solution(5162885880522562663)
XLA Ops:
  0.6 87.9 %shard_map.94 = (bf16[4096,128]{1,0:T(8,128)(2,1)}, bf16[256,128]{1,0:T(8,128)(2,1)}, bf16[256,128]{1,0:T(8,128)(2,1)}) custom-call(s32[32]{0:T(128)} %starts.1, bf16[4096,128]{1,0:T(8,128)(2,1)} %bitcast.9, bf16[256,128]{1,0:T(8,128)(2,1)} %bitcast.13, bf16[256,128]{1,0:T(8,128)(2,1)} %bitcast.14, bf16[4096,128]{1,0:T(8,128)(2,1)} %bitcast.10, ...), custom_call_target="tpu_custom_call" | custom-call | tf_op jit(solution)/shard_map/pallas_call | solution.py:334
  88.6 0.0 copy-start.1
  88.6 2.4 %copy.13 = bf16[1,256,16,128]{3,2,1,0:T(8,128)(2,1)} copy(bf16[1,256,16,128]{3,2,1,0:T(8,128)(2,1)} %bitcast.12) | data formatting | bytes 2097152
  91.0 0.0 copy-done.1
  91.0 0.0 copy-start
  91.0 0.6 copy.14
  91.6 0.2 copy-done
  91.9 0.6 copy.15
Async XLA Ops:
  88.6 2.4 %copy-start.1 = (bf16[256,128]{1,0:T(8,128)(2,1)S(1)}, bf16[256,128]{1,0:T(8,128)(2,1)}, u32[]{:S(2)}) copy-start(bf16[256,128]{1,0:T(8,128)(2,1)} %get-tuple-element.7) | copy-start | bytes 196612
  91.0 0.9 copy-start

commit v2 on v1

--- a/solution.py
+++ b/solution.py
@@ -10,6 +10,7 @@
 FAR = 1e30
 MESH = pl.DeviceIdType.MESH
 PHASES = 2
+CUT = 6
 
 
 def nn(a, b):
@@ -54,7 +55,7 @@
     half_rows, head = qc.shape[0], qc.shape[1] // 2
     span = kv.shape[1] // 2
     scale = head ** -0.5
-    step = half_rows // PHASES
+    edges = (0, half_rows * CUT // 16, half_rows)
     zh, y, core = me // 8, (me // 2) % 4, me % 2
 
     def at(dz, dy, dc):
@@ -73,6 +74,9 @@
     y_peers = [{"ctx": at(0, dy, 0)} for dy in (1, 2, 3)]
     before = {"section": (sec + sections - 1) % sections}
     after = {"section": (sec + 1) % sections}
+
+    def rows_of(phase):
+        return pl.ds(edges[phase], edges[phase + 1] - edges[phase])
 
     local = [
         pltpu.make_async_copy(k, kv.at[me, :, pl.ds(0, head)], in_s.at[0]),
@@ -92,18 +96,6 @@
         pl.semaphore_signal(barrier, inc=1, device_id=peer, device_id_type=MESH)
     pl.semaphore_wait(barrier, len(peers))
 
-    grads = []
-    for phase in range(PHASES):
-        for half in range(2):
-            n = phase * 2 + half
-            grads.append(
-                remote(
-                    g.at[pl.ds(half * half_rows + phase * step, step), :],
-                    dc.at[pl.ds(phase * step, step), pl.ds(half * head, head)],
-                    grad_s.at[n], grad_r.at[n], before,
-                )
-            )
-            grads[-1].start()
     for copy in local[:2]:
         copy.wait()
 
@@ -115,7 +107,6 @@
             out.append(
                 remote(kv.at[shard], kv.at[shard], kv_s.at[base + n], kv_r.at[first + slot], peer)
             )
-            out[-1].start()
         return out
 
     def arrived(j):
@@ -127,8 +118,24 @@
         return remote(spot, spot, fwd_s.at[j], kv_r.at[j + 4], core_peer)
 
     z_copy = remote(kv.at[me], kv.at[me], kv_s.at[8], kv_r.at[8], z_peer)
-    z_copy.start()
-    kv_copies = [z_copy, *spread(me, 0, 0)]
+    grads = []
+    for phase in range(PHASES):
+        for half in range(2):
+            n = phase * 2 + half
+            grads.append(
+                remote(
+                    g.at[pl.ds(half * half_rows + edges[phase], edges[phase + 1] - edges[phase]), :],
+                    dc.at[rows_of(phase), pl.ds(half * head, head)],
+                    grad_s.at[n], grad_r.at[n], before,
+                )
+            )
+            grads[-1].start()
+        if phase == 0:
+            z_copy.start()
+    kv_copies = [*spread(me, 0, 0)]
+    for copy in kv_copies:
+        copy.start()
+    kv_copies += [z_copy, *spread(index_of(8), 4, 8)]
 
     dq[...] = jnp.zeros_like(dq)
     for copy in local[2:]:
@@ -151,15 +158,10 @@
     for j in (1, 3, 2):
         arrived(j)
         forward(j).start()
-    arrived(8)
-    kv_copies += spread(index_of(8), 4, 8)
 
     zero = jnp.zeros((span, head), bf16)
     low_start = starts[2 * me]
     ones = jnp.ones((8, head), bf16)
-
-    def rows_of(phase):
-        return pl.ds(phase * step, step)
 
     def start_phase(phase):
         rows = rows_of(phase)
@@ -175,9 +177,9 @@
     def diagonal(phase):
         rows = rows_of(phase)
         token = lax.shift_right_logical(
-            lax.broadcasted_iota(jnp.int32, (span, step), 1), (half_rows // span).bit_length() - 1
-        ) + phase * (step * span // half_rows)
-        mask = lax.broadcasted_iota(jnp.int32, (span, step), 0) <= token
+            lax.broadcasted_iota(jnp.int32, (span, rows.size), 1), (half_rows // span).bit_length() - 1
+        ) + edges[phase] * span // half_rows
+        mask = lax.broadcasted_iota(jnp.int32, (span, rows.size), 0) <= token
         k_a, k_b = kv[me, :span, :head], kv[me, span:, :head]
         v_a, v_b = kv[me, :span, head:], kv[me, span:, head:]
         dk, dv = attend(
@@ -217,8 +219,9 @@
 
     def finish_rows(phase):
         for half in range(2):
-            part = dq[half * head : (half + 1) * head, phase * step : (phase + 1) * step]
-            dq_out[pl.ds(half * half_rows + phase * step, step), :] = (part.T * scale).astype(bf16)
+            low, high = edges[phase], edges[phase + 1]
+            part = dq[half * head : (half + 1) * head, low:high]
+            dq_out[pl.ds(half * half_rows + low, high - low), :] = (part.T * scale).astype(bf16)
 
     start_phase(0)
     acc[0] = diagonal(0)
@@ -233,6 +236,12 @@
         @pl.when(jnp.logical_and(j >= 9, j < 12))
         def _():
             forward(j).start()
+
+        @pl.when(j == 4)
+        def _():
+            arrived(8)
+            for copy in spread(index_of(8), 4, 8):
+                copy.start()
 
         terms = shard_terms(j, 0)
 
@@ -321,6 +330,12 @@
         if n % 4:
             sum2(n).wait_send()
     z_sum.wait_send()
+
+
+def hand_over(dq, dk, dv, dq_out, dk_out, dv_out):
+    dq_out[...] = dq[...]
+    dk_out[...] = dk[...]
+    dv_out[...] = dv[...]
 
 
 def body(queries, keys, values, outputs, grad_held, lse, span_start):
@@ -371,6 +386,16 @@
         outputs.reshape(2 * rows, head),
         lse[0],
     )
+    parts = 4
+    big = pl.BlockSpec((2 * rows // parts, head), lambda i: (i, 0))
+    small = pl.BlockSpec((tokens // parts, head), lambda i: (i, 0))
+    dq, dk, dv = pl.pallas_call(
+        hand_over,
+        grid=(parts,),
+        out_shape=tuple(jax.ShapeDtypeStruct(x.shape, x.dtype) for x in (dq, dk, dv)),
+        in_specs=[big, small, small],
+        out_specs=(big, small, small),
+    )(dq, dk, dv)
     return dq.reshape(1, tokens, heads, head), dk[None], dv[None]
 
 

time: 92.7 us -> 72.4 us (0.78)
  Pallas kernels: 87.9 us -> 71.4 us
  local copies, waits for them, and re-layouts: 3.9 us -> 0 us
    pallas_call x1, Pallas kernels: 87.9 us -> 68 us  [body(): pl.pallas_call(kernel, out_shape=(jax.ShapeDtypeStruct((2 * rows, head),...]
    unnamed x7 -> x0, local copies, waits for them, and re-layouts: 3.9 us -> none
    pallas_call x0 -> x1, Pallas kernels: none -> 3.43 us  [body(): pl.pallas_call(hand_over, grid=(parts,), out_shape=tuple((jax.ShapeDtypeS...]
where the time goes in v2:
time: 72.4 us; the launch traced here: 72.1 us
  Pallas kernels  71.4 us (99%)
    pallas_call x1, Pallas kernels, body(): pl.pallas_call(kernel, out_shape=(jax.ShapeDtypeStruct((2 * rows, head),...  68 us
    pallas_call x1, Pallas kernels, body(): pl.pallas_call(hand_over, grid=(parts,), out_shape=tuple((jax.ShapeDtypeS...  3.43 us

profile of v2, /device:TPU:1, one launch (start us, length us, event | category | flops | bytes accessed | tf_op | source)
XLA Modules:
  0.0 72.1 jit_solution(8707834553645539788)
XLA Ops:
  0.6 68.0 %shard_map.94 = (bf16[4096,128]{1,0:T(8,128)(2,1)}, bf16[256,128]{1,0:T(8,128)(2,1)}, bf16[256,128]{1,0:T(8,128)(2,1)}) custom-call(s32[32]{0:T(128)} %starts.1, bf16[4096,128]{1,0:T(8,128)(2,1)} %bitcast.9, bf16[256,128]{1,0:T(8,128)(2,1)} %bitcast.12, bf16[256,128]{1,0:T(8,128)(2,1)} %bitcast.13, bf16[4096,128]{1,0:T(8,128)(2,1)} %bitcast.10, ...), custom_call_target="tpu_custom_call" | custom-call | tf_op jit(solution)/shard_map/pallas_call | solution.py:349
  68.6 3.4 %shard_map.95 = (bf16[4096,128]{1,0:T(8,128)(2,1)}, bf16[256,128]{1,0:T(8,128)(2,1)}, bf16[256,128]{1,0:T(8,128)(2,1)}) custom-call(bf16[4096,128]{1,0:T(8,128)(2,1)} %get-tuple-element.9.dq, bf16[256,128]{1,0:T(8,128)(2,1)} %get-tuple-element.10.dk, bf16[256,128]{1,0:T(8,128)(2,1)} %get-tuple-element.11.dv), custom_call_target="tpu_custom_call" | custom-call | tf_op jit(solution)/shard_map/pallas_call | solution.py:392
